TPU v7x, 256 devices: a whole 4x4x8 slice. The times are simulated.
256 devices in a mesh: dp: 8 (over z), tensor: 32 (over y, x, core).
Axes of the slice: x: 4, y: 4, z: 8, core: 2. Of those that a mesh axis runs over, the one named last changes fastest.
Arguments:
- hidden: bfloat16 [16384, 1536], P(('dp', 'tensor')), parts along dimension 0, may hold values from -6 to 6
- segment_ids: int32 [16384], P('dp'), parts along dimension 0, may hold values from 0 to 5, never falling along the last dimension, each value on 1 to 1024 neighbouring positions
- routes: int32 [16384, 8], P(('dp', 'tensor')), parts along dimension 0, may hold values from 0 to 39, all different within a row; in each aligned block of 512 rows (0 to 511, 512 to 1023, ...) at most 204 rows name the same one
- route_weights: bfloat16 [16384, 8], P(('dp', 'tensor')), parts along dimension 0, may hold values from 0.099609375 to 1
- attn_gain: float32 [1536], replicated, may hold values from 0.1 to 1.9
- w_qkv: bfloat16 [1536, 2560], P(None, 'tensor')
- w_out: bfloat16 [1536, 1536], P(None, 'tensor'), may hold values from -0.15625 to 0.15625
- ffn_gain: float32 [1536], replicated, may hold values from 0.1 to 1.9
- w_gate_up: bfloat16 [160, 1536, 256], P('tensor'), may hold values from -0.15625 to 0.15625
- w_down: bfloat16 [160, 128, 1536], P('tensor'), may hold values from -0.25 to 0.25
Outputs:
- after_attention: bfloat16 [16384, 1536], P(('dp', 'tensor')), parts along dimension 0
- hidden_out: bfloat16 [16384, 1536], P(('dp', 'tensor')), parts along dimension 0
- kv_cache: bfloat16 [32, 4096, 128], P('tensor', 'dp'), parts along dimension 1
There are 8 independent parts, one for each index of `dp`. A program takes and returns all parts, laid end to end along the dimension named above; an argument that names none is the same for every part. Nothing has to cross between parts.
Inputs may be any that keep to these rules, and one draw needn't show every extreme that they name: `segment_ids`: prompt numbers never fall along the sequence; each prompt has 1 to 1024 tokens, one exactly 1024. `routes`: each token names 8 different experts. In each aligned block of 512 tokens no expert is named by more than 204 tokens, a bound that some block reaches.
All inputs are finite; a program needn't handle non-finite values.
Results may differ from a plain program's by a relative error of at most 0.0075.
Values may be sent and summed in bfloat16 or wider, within the bound.
A program may use at most 128 MiB of HBM per device.

v0:
```python
import math
import jax
import jax.numpy as jnp
from jax import lax
from jax.sharding import PartitionSpec as P

KVH = 8
HD = 64
GQ = 3
attn_scale = 0.015625
residual_scale = 0.22
rope_base = 10000.0
norm_eps = 1e-06
masked_floor = -1e30


def partner(value, axis, apart):
    mask = 2**apart
    pairs = [(source, source ^ mask) for source in range(lax.axis_size(axis))]
    return lax.ppermute(value, axis, pairs)


def rms_norm(row_block, gain_row):
    widened = row_block.astype(jnp.float32)
    mean_square = jnp.mean(widened * widened, axis=-1, keepdims=True)
    return (widened * lax.rsqrt(mean_square + norm_eps) * gain_row).astype(jnp.bfloat16)


def segment_starts(segment_ids):
    places = jnp.arange(segment_ids.shape[0], dtype=jnp.int32)
    earlier = jnp.concatenate([segment_ids[:1] - 1, segment_ids[:-1]])
    boundary = jnp.where(segment_ids != earlier, places, jnp.zeros_like(places))
    return lax.cummax(boundary, axis=0)


def rotate(vectors, positions):
    half_width = vectors.shape[-1] // 2
    freq_steps = jnp.arange(half_width, dtype=jnp.float32)
    frequency = jnp.exp(freq_steps * (-2.0 * math.log(rope_base) / vectors.shape[-1]))
    angles = positions.astype(jnp.float32)[:, None] * frequency[None, :]
    cosine = jnp.cos(angles)[:, None, :]
    sine_part = jnp.sin(angles)[:, None, :]
    first_half = vectors[..., :half_width]
    second_half = vectors[..., half_width:]
    return jnp.concatenate(
        [
            first_half * cosine - second_half * sine_part,
            second_half * cosine + first_half * sine_part,
        ],
        axis=-1,
    )


def gather_levels(parts, level_bits, join_axes, sender):
    index_now = lax.axis_index("tensor")
    for level_bit in level_bits:
        arrived = sender(parts, level_bit)
        is_upper = index_now >> level_bit & 1 == 1
        joined_parts = []
        for own_part, peer_part, join_axis in zip(parts, arrived, join_axes):
            lower_first = jnp.concatenate([own_part, peer_part], join_axis)
            upper_first = jnp.concatenate([peer_part, own_part], join_axis)
            joined_parts.append(jnp.where(is_upper, upper_first, lower_first))
        parts = tuple(joined_parts)
    return parts


def fold_levels(partial_sum, level_bits, sender):
    index_now = lax.axis_index("tensor")
    for level_bit in reversed(level_bits):
        half_rows = partial_sum.shape[0] // 2
        lower_rows = partial_sum[:half_rows]
        upper_rows = partial_sum[half_rows:]
        is_upper = index_now >> level_bit & 1 == 1
        kept_rows = jnp.where(is_upper, upper_rows, lower_rows)
        sent_rows = jnp.where(is_upper, lower_rows, upper_rows)
        partial_sum = kept_rows + sender(sent_rows, level_bit)
    return partial_sum


def project_pairs(row_block, w_pairs, positions):
    head_size = w_pairs.shape[1] // 2
    paired = jnp.dot(row_block, w_pairs, preferred_element_type=jnp.float32)
    rotated = rotate(paired[:, None, :head_size], positions)[:, 0]
    return jnp.concatenate([rotated, paired[:, head_size:]], axis=1).astype(jnp.bfloat16)


def expert_term(inputs, routes, route_weights, gate_up, down_proj, first_expert, capacity):
    row_count = inputs.shape[0]
    model_width = inputs.shape[1]
    expert_count = gate_up.shape[0]
    inner_width = down_proj.shape[1]
    expert_ids = first_expert + jnp.arange(expert_count, dtype=jnp.int32)
    matches = routes[:, None, :] == expert_ids[None, :, None]
    chosen = jnp.any(matches, axis=2)
    shares = jnp.sum(jnp.where(matches, route_weights.astype(jnp.float32)[:, None, :], 0.0), axis=2)
    ranks = jnp.cumsum(chosen.astype(jnp.int32), axis=0) - 1
    targets = jnp.where(chosen, ranks, capacity)
    row_ids = jnp.broadcast_to(
        jnp.arange(row_count, dtype=jnp.int32)[:, None], (row_count, expert_count)
    )
    column_ids = jnp.broadcast_to(
        jnp.arange(expert_count, dtype=jnp.int32)[None, :], (row_count, expert_count)
    )
    slot_table = (
        jnp.full((expert_count, capacity + 1), row_count, jnp.int32)
        .at[column_ids, targets]
        .set(row_ids)[:, :capacity]
    )
    padded_in = jnp.concatenate([inputs, jnp.zeros((1, model_width), inputs.dtype)], axis=0)
    padded_share = jnp.concatenate([shares, jnp.zeros((1, expert_count), jnp.float32)], axis=0)
    picked = padded_in[slot_table]
    slot_share = jnp.take_along_axis(padded_share.T, slot_table, axis=1)
    gate_up_out = jnp.einsum("ecd,edf->ecf", picked, gate_up, preferred_element_type=jnp.float32)
    inner_act = (
        jax.nn.silu(gate_up_out[..., :inner_width]) * gate_up_out[..., inner_width:]
    ).astype(jnp.bfloat16)
    produced = (
        jnp.einsum("ecf,efd->ecd", inner_act, down_proj, preferred_element_type=jnp.float32)
        * slot_share[..., None]
    )
    summed = (
        jnp.zeros((row_count + 1, model_width), jnp.float32)
        .at[slot_table.reshape(-1)]
        .add(produced.reshape(-1, model_width))
    )
    return summed[:row_count]


def on_device(
    hidden, segment_ids, routes, route_weights, attn_gain, w_qkv, w_out, ffn_gain, w_gate_up, w_down
):
    device_count = lax.axis_size("tensor")
    quarters = device_count // KVH
    index_now = lax.axis_index("tensor")
    quarter_index = index_now // KVH
    group_index = index_now % KVH
    group_bits = list(range(KVH.bit_length() - 1))
    quarter_bits = list(range(len(group_bits), device_count.bit_length() - 1))
    seq_len = segment_ids.shape[0]
    rows_quarter = seq_len // quarters
    model_width = hidden.shape[1]
    starts = segment_starts(segment_ids)
    positions = jnp.arange(seq_len, dtype=jnp.int32) - starts
    own_positions = lax.dynamic_slice_in_dim(
        positions, quarter_index * rows_quarter, rows_quarter, 0
    )
    normed = rms_norm(hidden, attn_gain)
    qkv_width = w_qkv.shape[1]
    joined = jnp.concatenate([w_qkv, w_out], axis=1)
    (gathered_cols,) = gather_levels(
        (joined,),
        quarter_bits,
        (1,),
        lambda payload, level_bit: (partner(payload[0], "tensor", level_bit),),
    )
    by_quarter = gathered_cols.reshape(model_width, quarters, joined.shape[1])
    w_group = by_quarter[:, :, :qkv_width].reshape(model_width, quarters * qkv_width)
    w_attn_out = by_quarter[:, :, qkv_width:].reshape(model_width, GQ * HD)
    w_query = w_group[:, : GQ * HD]
    w_pairs = w_group[:, GQ * HD :]
    all_rows = lax.all_gather(normed, "tensor", axis=0, tiled=True)
    own_rows = lax.dynamic_slice_in_dim(all_rows, quarter_index * rows_quarter, rows_quarter, 0)
    key_values = project_pairs(all_rows, w_pairs, positions)
    kv_block = lax.dynamic_slice_in_dim(key_values, quarter_index * rows_quarter, rows_quarter, 0)
    query_proj = jnp.dot(own_rows, w_query, preferred_element_type=jnp.float32).reshape(
        rows_quarter, GQ, HD
    )
    queries_heads = rotate(query_proj, own_positions).astype(jnp.bfloat16).transpose(1, 0, 2)
    block_rows = min(256, rows_quarter)
    key_block = min(512, seq_len)

    def attend(block_number):
        first_row = block_number * block_rows
        block_queries = lax.dynamic_slice_in_dim(queries_heads, first_row, block_rows, 1).reshape(
            GQ * block_rows, HD
        )
        first_place = quarter_index * rows_quarter + first_row
        query_places = first_place + jnp.arange(block_rows, dtype=jnp.int32)
        query_starts = lax.dynamic_slice_in_dim(starts, first_place, block_rows, 0)
        lowest = query_starts[0] // key_block
        highest = (first_place + block_rows - 1) // key_block + 1

        def step_keys(key_number, loop_state):
            row_peak, totals, accumulated = loop_state
            key_offset = key_number * key_block
            block_pairs = lax.dynamic_slice_in_dim(key_values, key_offset, key_block, 0)
            key_places = key_offset + jnp.arange(key_block, dtype=jnp.int32)
            allowed = (key_places[None, :] <= query_places[:, None]) & (
                key_places[None, :] >= query_starts[:, None]
            )
            scores = (
                lax.dot_general(
                    block_queries,
                    block_pairs[:, :HD],
                    (((1,), (1,)), ((), ())),
                    preferred_element_type=jnp.float32,
                )
                * attn_scale
            )
            scores = jnp.where(jnp.tile(allowed, (GQ, 1)), scores, -jnp.inf)
            new_peak = jnp.maximum(row_peak, jnp.max(scores, axis=1))
            weights = jnp.exp(scores - new_peak[:, None])
            factor = jnp.exp(row_peak - new_peak)
            totals = totals * factor + jnp.sum(weights, axis=1)
            accumulated = accumulated * factor[:, None] + jnp.dot(
                weights.astype(jnp.bfloat16),
                block_pairs[:, HD:],
                preferred_element_type=jnp.float32,
            )
            return (new_peak, totals, accumulated)

        start_state = (
            jnp.full((GQ * block_rows,), masked_floor, jnp.float32),
            jnp.zeros((GQ * block_rows,), jnp.float32),
            jnp.zeros((GQ * block_rows, HD), jnp.float32),
        )
        row_peak, totals, accumulated = lax.fori_loop(lowest, highest, step_keys, start_state)
        mixed = (accumulated / totals[:, None]).astype(jnp.bfloat16).reshape(GQ, block_rows, HD)
        return mixed.transpose(1, 0, 2).reshape(block_rows, GQ * HD)

    attended = lax.map(attend, jnp.arange(rows_quarter // block_rows, dtype=jnp.int32)).reshape(
        rows_quarter, GQ * HD
    )
    partial_proj = lax.dot_general(
        attended, w_attn_out, (((1,), (1,)), ((), ())), preferred_element_type=jnp.float32
    )
    projection = fold_levels(
        partial_proj,
        group_bits,
        lambda sent_rows, level_bit: partner(
            sent_rows.astype(jnp.bfloat16), "tensor", level_bit
        ).astype(sent_rows.dtype),
    )
    after_attention = (hidden.astype(jnp.float32) + residual_scale * projection).astype(
        jnp.bfloat16
    )
    expert_in = rms_norm(after_attention, ffn_gain)
    local_experts = w_gate_up.shape[0]
    capacity = 2 * rows_quarter // 5
    rows_all, routes_all, shares_all = (
        lax.all_gather(expert_in, "tensor", axis=0, tiled=True),
        lax.all_gather(routes, "tensor", axis=0, tiled=True),
        lax.all_gather(route_weights, "tensor", axis=0, tiled=True),
    )
    expert_part = expert_term(
        rows_all,
        routes_all,
        shares_all,
        w_gate_up,
        w_down,
        group_index * local_experts,
        quarters * capacity,
    )
    expert_sum = lax.psum_scatter(
        expert_part.astype(jnp.bfloat16), "tensor", scatter_dimension=0, tiled=True
    ).astype(jnp.float32)
    hidden_out = (after_attention.astype(jnp.float32) + residual_scale * expert_sum).astype(
        jnp.bfloat16
    )
    return (after_attention, hidden_out, kv_block[None])


def solution(mesh):
    placed = (
        P(("dp", "tensor"), None),
        P("dp"),
        P(("dp", "tensor"), None),
        P(("dp", "tensor"), None),
        P(),
        P(None, "tensor"),
        P(None, "tensor"),
        P(),
        P("tensor", None, None),
        P("tensor", None, None),
    )
    return jax.shard_map(
        on_device,
        mesh=mesh,
        in_specs=placed,
        out_specs=(P(("dp", "tensor"), None), P(("dp", "tensor"), None), P("tensor", "dp", None)),
        check_vma=False,
    )
```

profile of v0, /device:TPU:2, one launch (start us, length us, event | category | flops | bytes accessed | tf_op | source)
XLA Modules:
  0.0 499.2 jit_solution(2245536383037473471)
XLA Ops:
  8.4 1.7 fusion.19
  11.3 1.7 collective-permute-start
  16.1 6.1 %collective-permute-done = bf16[1536,128]{0,1:T(8,128)(2,1)S(1)} collective-permute-done((bf16[1536,128]{0,1:T(8,128)(2,1)S(1)}, bf16[1536,128]{0,1:T(8,128)(2,1)S(1)}, u32[]{:S(2)}, u32[]{:S(2)}) %collective-permute-start) | collective-permute-done | bytes 393248 | tf_op jit(solution)/shard_map/ppermute | solution.py:20
  23.6 3.3 collective-permute-start.1
  27.1 1.7 multiply_cosine_fusion.1
  28.8 18.0 %collective-permute-done.1 = bf16[1536,256]{0,1:T(8,128)(2,1)S(1)} collective-permute-done((bf16[1536,256]{0,1:T(8,128)(2,1)S(1)}, bf16[1536,256]{0,1:T(8,128)(2,1)S(1)}, u32[]{:S(2)}, u32[]{:S(2)}) %collective-permute-start.1) | collective-permute-done | bytes 786464 | tf_op jit(solution)/shard_map/ppermute | solution.py:20
  48.0 30.3 %all-gather.5.cloned.1.call-done = bf16[2048,1536]{1,0:T(8,128)(2,1)} async-done(((bf16[64,1536]{1,0:T(8,128)(2,1)}), bf16[2048,1536]{1,0:T(8,128)(2,1)}) %all-gather.5.cloned.1.call-update) | async-done | bytes 6291472 | tf_op jit(solution)/shard_map/all_gather | solution.py:162
  78.3 4.9 fusion.25
  83.3 2.1 fusion.12
  89.6 2.1 copy.61
  93.3 14.6 %while.59 = (s32[]{:T(128)}, bf16[2,256,192]{1,2,0:T(8,128)(2,1)}, s32[2]{0:T(128)S(1)}, s32[]{:T(128)}, s32[2048]{0:T(1024)S(1)}, /*index=5*/bf16[3,512,64]{2,1...) while((s32[]{:T(128)}, bf16[2,256,192]{1,2,0:T(8,128)(2,1)}, ...), condition=%wide.region_8.9_spmd, body=%wide.region_3.8_spmd.sunk | while | flops 104007976 | bytes 10327068 | solution.py:222
  97.8 2.0 while.60
  105.0 2.0 while.60
  108.8 1.7 fusion.47
  110.5 1.7 copy-done.1
  112.3 2.1 collective-permute-start.2
  114.4 19.2 %collective-permute-done.2 = bf16[256,1536]{1,0:T(8,128)(2,1)} collective-permute-done((bf16[256,1536]{1,0:T(8,128)(2,1)S(1)}, bf16[256,1536]{1,0:T(8,128)(2,1)}, u32[]{:S(2)}, u32[]{:S(2)}) %collective-permute-start.2) | collective-permute-done | bytes 786464 | tf_op jit(solution)/shard_map/ppermute | solution.py:20
  133.7 2.5 convert_add_fusion
  137.0 1.5 collective-permute-start.3
  138.5 9.2 %collective-permute-done.3 = bf16[128,1536]{1,0:T(8,128)(2,1)} collective-permute-done((bf16[128,1536]{1,0:T(8,128)(2,1)}, bf16[128,1536]{1,0:T(8,128)(2,1)}, u32[]{:S(2)}, u32[]{:S(2)}) %collective-permute-start.3) | collective-permute-done | bytes 393248 | tf_op jit(solution)/shard_map/ppermute | solution.py:20
  151.5 30.1 %all-gather.1 = bf16[32,64,8]{1,2,0:T(8,128)(2,1)S(1)} all-gather(bf16[1,64,8]{1,2,0:T(8,128)(2,1)S(1)} %bitcast.110), channel_id=1, replica_groups=mesh['dp'=8,'tensor'=32] {'tensor'}, dimensions={0}, use_global_device_ids=true | all-gather | bytes 33792 | tf_op jit(solution)/shard_map/all_gather | solution.py:244
  181.7 23.6 %all-gather = s32[32,64,8]{1,2,0:T(8,128)S(1)} all-gather(s32[1,64,8]{1,2,0:T(8,128)S(1)} %bitcast.109), channel_id=1, replica_groups=mesh['dp'=8,'tensor'=32] {'tensor'}, dimensions={0}, use_global_device_ids=true | all-gather | bytes 67584 | tf_op jit(solution)/shard_map/all_gather | solution.py:243
  211.2 37.9 %scatter_custom_fusion.1 = s32[4085]{0:T(1024)S(1)} fusion(s32[10240]{0:T(1024)S(1)} %reshape.400, s32[10240]{0:T(1024)S(1)} %reshape.402, s32[]{:T(128)} %constant.223.clone.1), kind=kCustom, calls=%fused_computation.101 | custom fusion | bytes 16344
  250.6 40.4 %gather_fusion.1 = f32[4080]{0:T(1024)S(1)} fusion(f32[5,2049]{0,1:T(8,128)S(1)} %pad_bitcast_fusion, s32[4080]{0:T(1024)S(1)} %reshape.386), kind=kCustom, calls=%fused_computation.1 | custom fusion | bytes 65280 | tf_op jit(solution)/shard_map/jit(take_along_axis)/gather | solution.py:113
  291.4 5.8 %concatenate.56 = bf16[2049,1536]{1,0:T(8,128)(2,1)} pad(bf16[2048,1536]{1,0:T(8,128)(2,1)} %all-gather.7.cloned.1.call-done, bf16[]{:T(256)} %constant.215.clone.1), padding=0_1x0_0 | pad | bytes 12585986 | tf_op jit(solution)/shard_map/concatenate | solution.py:110
  297.2 28.9 %gather_fusion = bf16[4080,1536]{1,0:T(8,128)(2,1)} fusion(bf16[2049,1536]{1,0:T(8,128)(2,1)} %concatenate.56, s32[4096]{0:T(1024)S(1)} %pad_clamp_fusion), kind=kCustom, calls=%fused_computation | custom fusion | bytes 25083840 | tf_op jit(solution)/shard_map/gather | solution.py:112
  326.2 7.6 %fusion.48 = f32[5,816,256]{2,1,0:T(8,128)S(1)} fusion(bf16[5,816,1536]{2,1,0:T(8,128)(2,1)} %bitcast.94, bf16[5,1536,256]{2,1,0:T(8,128)(2,1)} %param.22), kind=kOutput, calls=%fused_computation.117 | convolution fusion | flops 3208642560 | bytes 20643840 | tf_op jit(solution)/shard_map/ecd,edf->ecf/dot_general | solution.py:114
  333.8 10.1 %convolution_multiply_fusion = f32[5,816,1536]{2,1,0:T(8,128)} fusion(bf16[5,128,1536]{2,1,0:T(8,128)(2,1)S(1)} %copy-done, f32[5,816]{1,0:T(8,128)S(1)} %and_select_fusion, f32[5,816,256]{2,1,0:T(8,128)S(1)} %fusion.48), kind=kOutput, calls=%fused_computation.22 | convolution fusion | flops 1613721600 | bytes 31227840 | tf_op jit(solution)/shard_map/ecf,efd->ecd/dot_general | solution.py:119
  343.9 46.6 %scatter_custom_fusion = f32[2049,1536]{1,0:T(8,128)} fusion(s32[4080]{0:T(1024)S(1)} %bitcast.107, f32[4080,1536]{1,0:T(8,128)} %bitcast.92, f32[]{:T(128)} %constant.216.clone.1), kind=kCustom, calls=%fused_computation.24 | custom fusion | flops 6266880 | bytes 12589568 | tf_op jit(solution)/shard_map/scatter-add | solution.py:125
  390.5 8.0 %slice.188 = bf16[2048,1536]{1,0:T(8,128)(2,1)} slice(f32[2049,1536]{1,0:T(8,128)} %scatter_custom_fusion), slice={[0:2048], [0:1536]} | slice | bytes 12582912 | tf_op jit(solution)/shard_map/slice | solution.py:127
  400.3 90.7 %reduce-scatter.2.cloned.1.call-done = bf16[64,1536]{1,0:T(8,128)(2,1)} async-done(((bf16[2048,1536]{1,0:T(8,128)(2,1)}), bf16[64,1536]{1,0:T(8,128)(2,1)}) %reduce-scatter.2.cloned.1.call-update) | async-done | bytes 196624 | tf_op jit(solution)/shard_map/reduce_scatter | solution.py:255
  491.0 1.7 fusion.24
  (159 shorter events, 36.5 us)
Async XLA Ops:
  7.2 326.6 %copy-start = (bf16[5,128,1536]{2,1,0:T(8,128)(2,1)S(1)}, bf16[5,128,1536]{2,1,0:T(8,128)(2,1)}, u32[]{:S(2)}) copy-start(bf16[5,128,1536]{2,1,0:T(8,128)(2,1)} %param.23) | copy-start | bytes 5898244
  7.2 71.1 %all-gather.5.cloned.1.call-start = ((), (), s32[]{:S(2)}) async-start(), calls=%async_computation.1 | async-start | bytes 6488064 | tf_op jit(solution)/shard_map/all_gather | solution.py:162
  10.2 281.2 %all-gather.7.cloned.1.call-start = ((), (), s32[]{:S(2)}) async-start(), calls=%async_computation.2 | async-start | bytes 6488064 | tf_op jit(solution)/shard_map/all_gather | solution.py:242
  11.3 10.9 %collective-permute-start = (bf16[1536,128]{0,1:T(8,128)(2,1)S(1)}, bf16[1536,128]{0,1:T(8,128)(2,1)S(1)}, u32[]{:S(2)}, u32[]{:S(2)}) collective-permute-start(bf16[1536,128]{0,1:T(8,128)(2,1)S(1)} %pad_maximum_fusion.1), channel_id=1, source_target_pairs={{0,8},{1,9},{2,10},{3,11},{4,12},{5,13},{6,14},{7,15},{8,0},{9,1},... | collective-permute-start | bytes 1179656 | tf_op jit(solution)/shard_map/ppermute | solution.py:20
  23.6 23.2 %collective-permute-start.1 = (bf16[1536,256]{0,1:T(8,128)(2,1)S(1)}, bf16[1536,256]{0,1:T(8,128)(2,1)S(1)}, u32[]{:S(2)}, u32[]{:S(2)}) collective-permute-start(bf16[1536,256]{0,1:T(8,128)(2,1)S(1)} %maximum_select_fusion.1), channel_id=1, source_target_pairs={{0,16},{1,17},{2,18},{3,19},{4,20},{5,21},{6,22},{7,23},{8,24},{9,... | collective-permute-start | bytes 2359304 | tf_op jit(solution)/shard_map/ppermute | solution.py:20
  83.2 4.1 copy-start.2
  87.3 0.7 copy-start.4
  97.7 2.1 copy-start.8
  99.9 0.7 copy-start.9
  105.0 2.1 copy-start.8
  107.2 0.7 copy-start.9
  110.5 1.7 copy-start.1
  112.3 21.4 %collective-permute-start.2 = (bf16[256,1536]{1,0:T(8,128)(2,1)S(1)}, bf16[256,1536]{1,0:T(8,128)(2,1)}, u32[]{:S(2)}, u32[]{:S(2)}) collective-permute-start(bf16[256,1536]{1,0:T(8,128)(2,1)S(1)} %select_convert_fusion), channel_id=1, source_target_pairs={{0,4},{1,5},{2,6},{3,7},{4,0},{5,1},{6,2},{7,3},{8,12},{9,13},{10,... | collective-permute-start | bytes 2359304 | tf_op jit(solution)/shard_map/ppermute | solution.py:20
  137.0 10.7 %collective-permute-start.3 = (bf16[128,1536]{1,0:T(8,128)(2,1)}, bf16[128,1536]{1,0:T(8,128)(2,1)}, u32[]{:S(2)}, u32[]{:S(2)}) collective-permute-start(bf16[128,1536]{1,0:T(8,128)(2,1)} %select_convert_fusion.1), channel_id=1, source_target_pairs={{0,2},{1,3},{2,0},{3,1},{4,6},{5,7},{6,4},{7,5},{8,10},{9,11},{10,... | collective-permute-start | bytes 1179656 | tf_op jit(solution)/shard_map/ppermute | solution.py:20
  138.5 11.9 %copy-start.6 = (bf16[64,1536]{1,0:T(8,128)(2,1)S(1)}, bf16[64,1536]{1,0:T(8,128)(2,1)}, u32[]{:S(2)}) copy-start(bf16[64,1536]{1,0:T(8,128)(2,1)} %param.14) | copy-start | bytes 589828
  138.5 12.1 %copy-start.10 = (f32[1536]{0:T(1024)S(1)}, f32[1536]{0:T(1024)}, u32[]{:S(2)}) copy-start(f32[1536]{0:T(1024)} %param.21) | copy-start | bytes 18436
  138.5 13.0 %copy-start.12 = (bf16[64,8]{0,1:T(8,128)(2,1)S(1)}, bf16[64,8]{0,1:T(8,128)(2,1)}, u32[]{:S(2)}) copy-start(bf16[64,8]{0,1:T(8,128)(2,1)} %param.17) | copy-start | bytes 3076
  148.8 32.9 %copy-start.11 = (s32[64,8]{0,1:T(8,128)S(1)}, s32[64,8]{0,1:T(8,128)}, u32[]{:S(2)}) copy-start(s32[64,8]{0,1:T(8,128)} %param.16) | copy-start | bytes 6148
  148.8 58.8 %copy-start.14 = (s32[2]{0:T(128)S(1)}, s32[2]{0:T(128)}, u32[]{:S(2)}) copy-start(s32[2]{0:T(128)} %constant.248) | copy-start | bytes 28
  148.9 58.9 %copy-start.13 = (s32[2]{0:T(128)S(1)}, s32[2]{0:T(128)}, u32[]{:S(2)}) copy-start(s32[2]{0:T(128)} %constant.251) | copy-start | bytes 28
  148.9 1.5 collective-permute-start.4
  150.6 340.4 %copy-start.7 = (bf16[64,1536]{1,0:T(8,128)(2,1)}, bf16[64,1536]{1,0:T(8,128)(2,1)S(1)}, u32[]{:S(2)}) copy-start(bf16[64,1536]{1,0:T(8,128)(2,1)S(1)} %get-tuple-element.314) | copy-start | bytes 589828
  151.5 339.5 %reduce-scatter.2.cloned.1.call-start = ((), (), s32[]{:S(2)}) async-start(), calls=%async_computation.3 | async-start | bytes 6488064 | tf_op jit(solution)/shard_map/reduce_scatter | solution.py:255
  398.5 0.9 copy-start.3
  398.5 1.0 copy-start.5
Sparse Core Ops, SparseCore 0:
  11.1 67.1 all-gather.4
  151.6 60.2 all-gather.6
  398.6 92.2 reduce-scatter.1
where the time goes:
time: 500 us; the launch traced here: 499 us
  waiting for transfers between devices  175 us (35%)
  local copies, waits for them, and re-layouts  143 us (29%)
  other arithmetic  68.6 us (14%)
  blocking collectives  53.6 us (11%)
  matrix products  28.2 us (6%)
  between operations  14.8 us (3%)
  starting transfers between devices  8.83 us (2%)
  loops' own time  6.75 us (1%)
    reduce_scatter x1, waiting for transfers between devices, on_device(): lax.psum_scatter(expert_part.astype(jnp.bfloat16), 'tensor', scatter_dime...  90.7 us
    ppermute x5, waiting for transfers between devices, partner(): return lax.ppermute(value, axis, pairs)  53.9 us
    scatter-add x1, other arithmetic, expert_term(): summed = jnp.zeros((row_count + 1, model_width), jnp.float32).at[slot_tab...  46.6 us
    unnamed x33, local copies, waits for them, and re-layouts  45.8 us
    gather x3, local copies, waits for them, and re-layouts, expert_term(): slot_share = jnp.take_along_axis(padded_share.T, slot_table, axis=1)  40.6 us
    all_gather x1, waiting for transfers between devices, on_device(): all_rows = lax.all_gather(normed, 'tensor', axis=0, tiled=True)  30.3 us
    all_gather x1, blocking collectives, on_device(): lax.all_gather(route_weights, 'tensor', axis=0, tiled=True)  30.1 us
    gather x1, local copies, waits for them, and re-layouts, expert_term(): picked = padded_in[slot_table]  28.9 us
  transfers between devices with their start and end apart: 8, of which 7 were waited for; matrix products, arithmetic and copies ran while one was open for 19% of the time, Pallas kernels for 0%

commit v1 on v0

--- a/solution.py
+++ b/solution.py
@@ -159,7 +159,9 @@
     w_attn_out = by_quarter[:, :, qkv_width:].reshape(model_width, GQ * HD)
     w_query = w_group[:, : GQ * HD]
     w_pairs = w_group[:, GQ * HD :]
-    all_rows = lax.all_gather(normed, "tensor", axis=0, tiled=True)
+    all_rows = jnp.concatenate(
+        lax.all_to_all(jnp.stack([normed] * lax.axis_size("tensor")), "tensor", 0, 0), axis=0
+    )
     own_rows = lax.dynamic_slice_in_dim(all_rows, quarter_index * rows_quarter, rows_quarter, 0)
     key_values = project_pairs(all_rows, w_pairs, positions)
     kv_block = lax.dynamic_slice_in_dim(key_values, quarter_index * rows_quarter, rows_quarter, 0)

time: 500 us -> 544 us (1.088)
  waiting for transfers between devices: 175 us -> 209 us
  starting transfers between devices: 8.83 us -> 17.2 us
    ppermute x5, waiting for transfers between devices: 53.9 us -> 117 us  [partner(): return lax.ppermute(value, axis, pairs)]
    all_gather x1 -> x0, waiting for transfers between devices: 30.3 us -> none  [on_device(): all_rows = lax.all_gather(normed, 'tensor', axis=0, tiled=True)]
    all_to_all x0 -> x1, starting transfers between devices: none -> 7.8 us  [on_device(): lax.all_to_all(jnp.stack([normed] * lax.axis_size('tensor')), 'tensor', 0...]
    unnamed x33 -> x39, local copies, waits for them, and re-layouts: 45.8 us -> 45.8 us
  transfers between devices with their start and end apart: 8 -> 8, of which waited for: 7 -> 6; matrix products, arithmetic and copies ran while one was open for 19% -> 17% of each run, Pallas kernels for 0% -> 0%
where the time goes in v1:
time: 544 us; the launch traced here: 543 us
  waiting for transfers between devices  209 us (38%)
  local copies, waits for them, and re-layouts  146 us (27%)
  other arithmetic  64.9 us (12%)
  blocking collectives  55.5 us (10%)
  matrix products  28.2 us (5%)
  starting transfers between devices  17.2 us (3%)
  between operations  15.2 us (3%)
  loops' own time  6.79 us (1%)
    ppermute x5, waiting for transfers between devices, partner(): return lax.ppermute(value, axis, pairs)  117 us
    reduce_scatter x1, waiting for transfers between devices, on_device(): lax.psum_scatter(expert_part.astype(jnp.bfloat16), 'tensor', scatter_dime...  92.4 us
    scatter-add x1, other arithmetic, expert_term(): summed = jnp.zeros((row_count + 1, model_width), jnp.float32).at[slot_tab...  46.6 us
    unnamed x39, local copies, waits for them, and re-layouts  45.8 us
    gather x3, local copies, waits for them, and re-layouts, expert_term(): slot_share = jnp.take_along_axis(padded_share.T, slot_table, axis=1)  40.6 us
    all_gather x1, blocking collectives, on_device(): lax.all_gather(route_weights, 'tensor', axis=0, tiled=True)  31.4 us
    gather x1, local copies, waits for them, and re-layouts, expert_term(): picked = padded_in[slot_table]  28.9 us
    all_gather x1, blocking collectives, on_device(): lax.all_gather(routes, 'tensor', axis=0, tiled=True)  24.1 us
  transfers between devices with their start and end apart: 8, of which 6 were waited for; matrix products, arithmetic and copies ran while one was open for 17% of the time, Pallas kernels for 0%

profile of v1, /device:TPU:2, one launch (start us, length us, event | category | flops | bytes accessed | tf_op | source)
XLA Modules:
  0.0 543.4 jit_solution(6975249027761952776)
XLA Ops:
  9.5 3.4 stack.2
  12.8 7.8 %all-to-all-start = ((bf16[32,64,1536]{2,1,0:T(8,128)(2,1)}), bf16[32,64,1536]{2,1,0:T(8,128)(2,1)}, u32[]{:S(2)}, u32[]{:S(2)}) async-start(bf16[32,64,1536]{2,1,0:T(8,128)(2,1)} %stack.2), calls=%async_computation | async-start | bytes 12582912 | tf_op jit(solution)/shard_map/all_to_all | solution.py:163
  20.7 1.6 collective-permute-start
  24.1 75.2 %collective-permute-done = bf16[1536,128]{0,1:T(8,128)(2,1)S(1)} collective-permute-done((bf16[1536,128]{0,1:T(8,128)(2,1)S(1)}, bf16[1536,128]{0,1:T(8,128)(2,1)S(1)}, u32[]{:S(2)}, u32[]{:S(2)}) %collective-permute-start) | collective-permute-done | bytes 393248 | tf_op jit(solution)/shard_map/ppermute | solution.py:20
  99.4 2.8 collective-permute-start.1
  102.4 1.7 multiply_cosine_fusion.1
  104.1 15.8 %collective-permute-done.1 = bf16[1536,256]{0,1:T(8,128)(2,1)S(1)} collective-permute-done((bf16[1536,256]{0,1:T(8,128)(2,1)S(1)}, bf16[1536,256]{0,1:T(8,128)(2,1)S(1)}, u32[]{:S(2)}, u32[]{:S(2)}) %collective-permute-start.1) | collective-permute-done | bytes 786464 | tf_op jit(solution)/shard_map/ppermute | solution.py:20
  121.2 2.1 fusion.12
  123.2 4.9 fusion.25
  132.4 2.1 copy.61
  136.2 14.7 %while.59 = (s32[]{:T(128)}, bf16[2,256,192]{1,2,0:T(8,128)(2,1)}, s32[2]{0:T(128)S(1)}, s32[]{:T(128)}, s32[2048]{0:T(1024)S(1)}, /*index=5*/bf16[3,512,64]{2,1...) while((s32[]{:T(128)}, bf16[2,256,192]{1,2,0:T(8,128)(2,1)}, ...), condition=%wide.region_8.9_spmd, body=%wide.region_3.8_spmd.sunk | while | flops 104007976 | bytes 10327068 | solution.py:224
  140.7 2.0 while.60
  148.1 2.0 while.60
  151.8 1.7 fusion.47
  153.5 1.7 copy-done.1
  155.3 2.7 collective-permute-start.2
  158.0 17.1 %collective-permute-done.2 = bf16[256,1536]{1,0:T(8,128)(2,1)} collective-permute-done((bf16[256,1536]{1,0:T(8,128)(2,1)S(1)}, bf16[256,1536]{1,0:T(8,128)(2,1)}, u32[]{:S(2)}, u32[]{:S(2)}) %collective-permute-start.2) | collective-permute-done | bytes 786464 | tf_op jit(solution)/shard_map/ppermute | solution.py:20
  175.1 2.5 convert_add_fusion
  178.4 2.0 collective-permute-start.3
  180.4 7.4 %collective-permute-done.3 = bf16[128,1536]{1,0:T(8,128)(2,1)} collective-permute-done((bf16[128,1536]{1,0:T(8,128)(2,1)}, bf16[128,1536]{1,0:T(8,128)(2,1)}, u32[]{:S(2)}, u32[]{:S(2)}) %collective-permute-start.3) | collective-permute-done | bytes 393248 | tf_op jit(solution)/shard_map/ppermute | solution.py:20
  191.9 31.4 %all-gather.1 = bf16[32,64,8]{1,2,0:T(8,128)(2,1)S(1)} all-gather(bf16[1,64,8]{1,2,0:T(8,128)(2,1)S(1)} %bitcast.111), channel_id=1, replica_groups=mesh['dp'=8,'tensor'=32] {'tensor'}, dimensions={0}, use_global_device_ids=true | all-gather | bytes 33792 | tf_op jit(solution)/shard_map/all_gather | solution.py:246
  223.4 24.1 %all-gather = s32[32,64,8]{1,2,0:T(8,128)S(1)} all-gather(s32[1,64,8]{1,2,0:T(8,128)S(1)} %bitcast.110), channel_id=1, replica_groups=mesh['dp'=8,'tensor'=32] {'tensor'}, dimensions={0}, use_global_device_ids=true | all-gather | bytes 67584 | tf_op jit(solution)/shard_map/all_gather | solution.py:245
  253.4 37.9 %scatter_custom_fusion.1 = s32[4085]{0:T(1024)S(1)} fusion(s32[10240]{0:T(1024)S(1)} %reshape.406, s32[10240]{0:T(1024)S(1)} %reshape.408, s32[]{:T(128)} %constant.223.clone.1), kind=kCustom, calls=%fused_computation.101 | custom fusion | bytes 16344
  292.8 40.4 %gather_fusion.1 = f32[4080]{0:T(1024)S(1)} fusion(f32[5,2049]{0,1:T(8,128)S(1)} %pad_bitcast_fusion, s32[4080]{0:T(1024)S(1)} %reshape.392), kind=kCustom, calls=%fused_computation.1 | custom fusion | bytes 65280 | tf_op jit(solution)/shard_map/jit(take_along_axis)/gather | solution.py:113
  333.6 5.8 %concatenate.56 = bf16[2049,1536]{1,0:T(8,128)(2,1)} pad(bf16[2048,1536]{1,0:T(8,128)(2,1)} %all-gather.4.cloned.1.call-done, bf16[]{:T(256)} %constant.215.clone.1), padding=0_1x0_0 | pad | bytes 12585986 | tf_op jit(solution)/shard_map/concatenate | solution.py:110
  339.4 28.9 %gather_fusion = bf16[4080,1536]{1,0:T(8,128)(2,1)} fusion(bf16[2049,1536]{1,0:T(8,128)(2,1)} %concatenate.56, s32[4096]{0:T(1024)S(1)} %pad_clamp_fusion), kind=kCustom, calls=%fused_computation | custom fusion | bytes 25083840 | tf_op jit(solution)/shard_map/gather | solution.py:112
  368.4 7.6 %fusion.48 = f32[5,816,256]{2,1,0:T(8,128)S(1)} fusion(bf16[5,816,1536]{2,1,0:T(8,128)(2,1)} %bitcast.95, bf16[5,1536,256]{2,1,0:T(8,128)(2,1)} %param.22), kind=kOutput, calls=%fused_computation.117 | convolution fusion | flops 3208642560 | bytes 20643840 | tf_op jit(solution)/shard_map/ecd,edf->ecf/dot_general | solution.py:114
  376.0 10.1 %convolution_multiply_fusion = f32[5,816,1536]{2,1,0:T(8,128)} fusion(bf16[5,128,1536]{2,1,0:T(8,128)(2,1)S(1)} %copy-done, f32[5,816]{1,0:T(8,128)S(1)} %and_select_fusion, f32[5,816,256]{2,1,0:T(8,128)S(1)} %fusion.48), kind=kOutput, calls=%fused_computation.22 | convolution fusion | flops 1613721600 | bytes 31227840 | tf_op jit(solution)/shard_map/ecf,efd->ecd/dot_general | solution.py:119
  386.1 46.6 %scatter_custom_fusion = f32[2049,1536]{1,0:T(8,128)} fusion(s32[4080]{0:T(1024)S(1)} %bitcast.108, f32[4080,1536]{1,0:T(8,128)} %bitcast.93, f32[]{:T(128)} %constant.216.clone.1), kind=kCustom, calls=%fused_computation.24 | custom fusion | flops 6266880 | bytes 12589568 | tf_op jit(solution)/shard_map/scatter-add | solution.py:125
  432.7 8.0 %slice.188 = bf16[2048,1536]{1,0:T(8,128)(2,1)} slice(f32[2049,1536]{1,0:T(8,128)} %scatter_custom_fusion), slice={[0:2048], [0:1536]} | slice | bytes 12582912 | tf_op jit(solution)/shard_map/slice | solution.py:127
  442.5 92.4 %reduce-scatter.2.cloned.1.call-done = bf16[64,1536]{1,0:T(8,128)(2,1)} async-done(((bf16[2048,1536]{1,0:T(8,128)(2,1)}), bf16[64,1536]{1,0:T(8,128)(2,1)}) %reduce-scatter.2.cloned.1.call-update) | async-done | bytes 196624 | tf_op jit(solution)/shard_map/reduce_scatter | solution.py:257
  534.9 1.7 fusion.24
  (165 shorter events, 34.1 us)
Async XLA Ops:
  7.2 368.8 %copy-start = (bf16[5,128,1536]{2,1,0:T(8,128)(2,1)S(1)}, bf16[5,128,1536]{2,1,0:T(8,128)(2,1)}, u32[]{:S(2)}) copy-start(bf16[5,128,1536]{2,1,0:T(8,128)(2,1)} %param.23) | copy-start | bytes 5898244
  12.8 7.9 %copy-start.8 = (bf16[1536,80]{0,1:T(8,128)(2,1)S(1)}, bf16[1536,80]{0,1:T(8,128)(2,1)}, u32[]{:S(2)}) copy-start(bf16[1536,80]{0,1:T(8,128)(2,1)} %param.19) | copy-start | bytes 737284
  12.8 7.9 %copy-start.9 = (bf16[1536,48]{0,1:T(8,128)(2,1)S(1)}, bf16[1536,48]{0,1:T(8,128)(2,1)}, u32[]{:S(2)}) copy-start(bf16[1536,48]{0,1:T(8,128)(2,1)} %param.20) | copy-start | bytes 442372
  12.8 9.5 %copy-start.12 = (s32[2048]{0:T(1024)S(1)}, s32[2048]{0:T(1024)}, u32[]{:S(2)}) copy-start(s32[2048]{0:T(1024)} %param.15) | copy-start | bytes 24580
  12.8 108.3 %all-to-all-start = ((bf16[32,64,1536]{2,1,0:T(8,128)(2,1)}), bf16[32,64,1536]{2,1,0:T(8,128)(2,1)}, u32[]{:S(2)}, u32[]{:S(2)}) async-start(bf16[32,64,1536]{2,1,0:T(8,128)(2,1)} %stack.2), calls=%async_computation | async-start | bytes 12582912 | tf_op jit(solution)/shard_map/all_to_all | solution.py:163
  20.6 313.0 %all-gather.4.cloned.1.call-start = ((), (), s32[]{:S(2)}) async-start(), calls=%async_computation.2 | async-start | bytes 6488064 | tf_op jit(solution)/shard_map/all_gather | solution.py:244
  20.7 78.5 %collective-permute-start = (bf16[1536,128]{0,1:T(8,128)(2,1)S(1)}, bf16[1536,128]{0,1:T(8,128)(2,1)S(1)}, u32[]{:S(2)}, u32[]{:S(2)}) collective-permute-start(bf16[1536,128]{0,1:T(8,128)(2,1)S(1)} %pad_maximum_fusion.1), channel_id=1, source_target_pairs={{0,8},{1,9},{2,10},{3,11},{4,12},{5,13},{6,14},{7,15},{8,0},{9,1},... | collective-permute-start | bytes 1179656 | tf_op jit(solution)/shard_map/ppermute | solution.py:20
  99.4 20.6 %collective-permute-start.1 = (bf16[1536,256]{0,1:T(8,128)(2,1)S(1)}, bf16[1536,256]{0,1:T(8,128)(2,1)S(1)}, u32[]{:S(2)}, u32[]{:S(2)}) collective-permute-start(bf16[1536,256]{0,1:T(8,128)(2,1)S(1)} %maximum_select_fusion.1), channel_id=1, source_target_pairs={{0,16},{1,17},{2,18},{3,19},{4,20},{5,21},{6,22},{7,23},{8,24},{9,... | collective-permute-start | bytes 2359304 | tf_op jit(solution)/shard_map/ppermute | solution.py:20
  128.2 2.0 copy-start.2
  130.2 0.7 copy-start.4
  140.7 2.1 copy-start.10
  142.9 0.7 copy-start.11
  148.0 2.1 copy-start.10
  150.2 0.7 copy-start.11
  153.5 1.7 copy-start.1
  155.3 19.8 %collective-permute-start.2 = (bf16[256,1536]{1,0:T(8,128)(2,1)S(1)}, bf16[256,1536]{1,0:T(8,128)(2,1)}, u32[]{:S(2)}, u32[]{:S(2)}) collective-permute-start(bf16[256,1536]{1,0:T(8,128)(2,1)S(1)} %select_convert_fusion), channel_id=1, source_target_pairs={{0,4},{1,5},{2,6},{3,7},{4,0},{5,1},{6,2},{7,3},{8,12},{9,13},{10,... | collective-permute-start | bytes 2359304 | tf_op jit(solution)/shard_map/ppermute | solution.py:20
  178.4 9.4 %collective-permute-start.3 = (bf16[128,1536]{1,0:T(8,128)(2,1)}, bf16[128,1536]{1,0:T(8,128)(2,1)}, u32[]{:S(2)}, u32[]{:S(2)}) collective-permute-start(bf16[128,1536]{1,0:T(8,128)(2,1)} %select_convert_fusion.1), channel_id=1, source_target_pairs={{0,2},{1,3},{2,0},{3,1},{4,6},{5,7},{6,4},{7,5},{8,10},{9,11},{10,... | collective-permute-start | bytes 1179656 | tf_op jit(solution)/shard_map/ppermute | solution.py:20
  180.4 10.3 %copy-start.6 = (bf16[64,1536]{1,0:T(8,128)(2,1)S(1)}, bf16[64,1536]{1,0:T(8,128)(2,1)}, u32[]{:S(2)}) copy-start(bf16[64,1536]{1,0:T(8,128)(2,1)} %param.14) | copy-start | bytes 589828
  180.4 10.6 %copy-start.13 = (f32[1536]{0:T(1024)S(1)}, f32[1536]{0:T(1024)}, u32[]{:S(2)}) copy-start(f32[1536]{0:T(1024)} %param.21) | copy-start | bytes 18436
  180.4 11.4 %copy-start.15 = (bf16[64,8]{0,1:T(8,128)(2,1)S(1)}, bf16[64,8]{0,1:T(8,128)(2,1)}, u32[]{:S(2)}) copy-start(bf16[64,8]{0,1:T(8,128)(2,1)} %param.17) | copy-start | bytes 3076
  188.9 34.4 %copy-start.14 = (s32[64,8]{0,1:T(8,128)S(1)}, s32[64,8]{0,1:T(8,128)}, u32[]{:S(2)}) copy-start(s32[64,8]{0,1:T(8,128)} %param.16) | copy-start | bytes 6148
  188.9 60.9 %copy-start.17 = (s32[2]{0:T(128)S(1)}, s32[2]{0:T(128)}, u32[]{:S(2)}) copy-start(s32[2]{0:T(128)} %constant.248) | copy-start | bytes 28
  189.0 60.9 %copy-start.16 = (s32[2]{0:T(128)S(1)}, s32[2]{0:T(128)}, u32[]{:S(2)}) copy-start(s32[2]{0:T(128)} %constant.251) | copy-start | bytes 28
  189.0 1.7 collective-permute-start.4
  190.9 344.0 %copy-start.7 = (bf16[64,1536]{1,0:T(8,128)(2,1)}, bf16[64,1536]{1,0:T(8,128)(2,1)S(1)}, u32[]{:S(2)}) copy-start(bf16[64,1536]{1,0:T(8,128)(2,1)S(1)} %get-tuple-element.314) | copy-start | bytes 589828
  191.8 343.1 %reduce-scatter.2.cloned.1.call-start = ((), (), s32[]{:S(2)}) async-start(), calls=%async_computation.3 | async-start | bytes 6488064 | tf_op jit(solution)/shard_map/reduce_scatter | solution.py:257
  440.7 0.9 copy-start.3
  440.7 1.0 copy-start.5
Sparse Core Ops, SparseCore 0:
  191.9 63.8 all-gather.3
  440.9 94.0 reduce-scatter.1
